TPU v7x, 32 devices: a whole 2x2x4 slice. The times are simulated.
32 devices in a mesh: chan: 4 (over z), tile: 8 (over y, x, core).
Axes of the slice: x: 2, y: 2, z: 4, core: 2. Of those that a mesh axis runs over, the one named last changes fastest.
Arguments:
- visibility: bfloat16 [1024, 2, 1024], P('tile', None, 'chan'), may hold values from -6 to 6
- flags: int32 [1024, 1024], P('tile', 'chan'), may hold values 0 or 1
- u_index: int32 [1024], replicated, may hold values from 0 to 511
- v_index: int32 [1024], replicated, may hold values from 0 to 255
- fg_filter: bfloat16 [1024, 1024], replicated, may hold values from -1 to 1
Outputs:
- cleaned: float32 [1024, 2, 1024], P('tile', None, 'chan')
All inputs are finite; a program needn't handle non-finite values. No bound on the sum of `flags` on one device may be relied on, other than what follows from the above.
Results may differ from a plain program's by a relative error of at most 0.0029.
Values may be sent and summed in bfloat16 or wider, within the bound.
No kernel may reach another device: no remote copies, remote signals or barrier semaphores. Data moves between devices by JAX's collectives and lax.ppermute only.
A program may use at most 256 MiB of HBM per device.

v0:
```python
import math
import jax
import jax.numpy as jnp
from jax import lax
from jax.sharding import PartitionSpec as P

F = 1024
L = 512
M = 256
TWO_PI = 2.0 * math.pi
FINE_STEP = 8


def tables(grid_index, positions, period):
    turn_count = grid_index[:, None] * positions[None, :] % period
    angles = turn_count.astype(jnp.float32) * (TWO_PI / period)
    return (jnp.cos(angles).astype(jnp.bfloat16), jnp.sin(angles).astype(jnp.bfloat16))


def line_tables(u_rows, line_ids, chan_start, chan_count, chan_total, line_total):
    period = chan_total * line_total
    coarse_ids = (
        chan_total + chan_start + FINE_STEP * jnp.arange(chan_count // FINE_STEP, dtype=jnp.int32)
    )
    fine_ids = jnp.arange(FINE_STEP, dtype=jnp.int32)
    base = u_rows[:, None] * line_ids[None, :]
    coarse_turns = base[:, :, None] * coarse_ids[None, None, :] % period
    fine_turns = base[:, :, None] * fine_ids[None, None, :] % period
    coarse_angle = coarse_turns.astype(jnp.float32) * (TWO_PI / period)
    fine_angle = fine_turns.astype(jnp.float32) * (TWO_PI / period)
    coarse_cos = jnp.cos(coarse_angle)[:, :, :, None]
    coarse_sin = jnp.sin(coarse_angle)[:, :, :, None]
    fine_cos = jnp.cos(fine_angle)[:, :, None, :]
    fine_sin = jnp.sin(fine_angle)[:, :, None, :]
    whole_cos = coarse_cos * fine_cos - coarse_sin * fine_sin
    whole_sin = coarse_sin * fine_cos + coarse_cos * fine_sin
    shape = (u_rows.shape[0], line_ids.shape[0], chan_count)
    return (
        whole_cos.reshape(shape).astype(jnp.bfloat16),
        whole_sin.reshape(shape).astype(jnp.bfloat16),
    )


def predict(image_lines, cos_line, sin_line, cos_col, sin_col):
    line_count, chan_count, pixel_cols = image_lines.shape
    row_count = cos_col.shape[0]
    phase_both = jnp.concatenate([cos_col, sin_col], 0)
    hidden_sum = lax.dot_general(
        image_lines.reshape(line_count * chan_count, pixel_cols),
        phase_both,
        (((1,), (1,)), ((), ())),
        preferred_element_type=jnp.float32,
    )
    hidden_sum = hidden_sum.reshape(line_count, chan_count, 2, row_count)
    half_cos = hidden_sum[:, :, 0, :]
    half_sin = hidden_sum[:, :, 1, :]
    row_cos = jnp.transpose(cos_line.astype(jnp.float32), (1, 2, 0))
    row_sin = jnp.transpose(sin_line.astype(jnp.float32), (1, 2, 0))
    real_pred = jnp.sum(row_cos * half_cos - row_sin * half_sin, axis=0)
    imag_pred = -jnp.sum(row_sin * half_cos + row_cos * half_sin, axis=0)
    return jnp.transpose(jnp.stack([real_pred, imag_pred], 0), (2, 0, 1))


def local(visibility, flags, u_index, v_index, fg_filter):
    row_count = visibility.shape[0]
    chan_count = visibility.shape[2]
    total_rows = u_index.shape[0]
    line_count = L // lax.axis_size("tile")
    line_ids = lax.axis_index("tile") * line_count + jnp.arange(line_count, dtype=jnp.int32)
    chan_start = lax.axis_index("chan") * chan_count
    cos_line, sin_line = line_tables(u_index, line_ids, chan_start, chan_count, F, L)
    cos_col, sin_col = tables(v_index, jnp.arange(M, dtype=jnp.int32), 2 * M)
    weight = flags.astype(jnp.bfloat16)
    weighted = visibility * weight[:, None, :]
    shard_piece = lax.all_gather(weighted, "tile", axis=0, tiled=True)
    piece_rows = shard_piece.shape[0]
    line_cos = cos_line.astype(jnp.float32)
    line_sin = sin_line.astype(jnp.float32)
    real_part = shard_piece[:, 0, :].astype(jnp.float32)[:, None, :]
    imag_part = shard_piece[:, 1, :].astype(jnp.float32)[:, None, :]
    x_real = (real_part * line_cos - imag_part * line_sin).astype(jnp.bfloat16)
    x_imag = (real_part * line_sin + imag_part * line_cos).astype(jnp.bfloat16)
    stacked = jnp.concatenate([x_real, x_imag], 0).reshape(2 * piece_rows, line_count * chan_count)
    phase_cols = jnp.concatenate([cos_col, -sin_col], 0)
    dirty_sum = lax.dot_general(
        stacked, phase_cols, (((0,), (0,)), ((), ())), preferred_element_type=jnp.float32
    )
    dirty_image = (
        (dirty_sum * (1.0 / math.sqrt(total_rows)))
        .astype(jnp.bfloat16)
        .reshape(line_count, chan_count, M)
    )
    filtered = jnp.einsum(
        "fg,qgm->qfm",
        fg_filter,
        lax.all_to_all(dirty_image, "chan", split_axis=0, concat_axis=1, tiled=True),
        preferred_element_type=jnp.float32,
    ).astype(jnp.bfloat16)
    foreground = lax.all_to_all(filtered, "chan", split_axis=1, concat_axis=0, tiled=True)
    own_start = lax.axis_index("tile") * row_count
    u_owned = lax.dynamic_slice_in_dim(u_index, own_start, row_count, 0)
    v_owned = lax.dynamic_slice_in_dim(v_index, own_start, row_count, 0)
    full_cos, full_sin = line_tables(
        u_owned, jnp.arange(L, dtype=jnp.int32), chan_start, chan_count, F, L
    )
    own_cos, own_sin = tables(v_owned, jnp.arange(M, dtype=jnp.int32), 2 * M)
    zero_rows = jnp.zeros((row_count, 2, chan_count), jnp.float32)
    shard_piece = lax.all_gather(foreground, "tile", axis=0, tiled=True)
    piece_lines = shard_piece.shape[0]
    block_count = piece_lines // line_count
    blocks = shard_piece.reshape(block_count, line_count, chan_count, M)
    offsets = jnp.arange(block_count, dtype=jnp.int32) * line_count

    def one_block(carried, scan_item):
        block_lines, offset = scan_item
        block_cos = lax.dynamic_slice_in_dim(full_cos, offset, line_count, 1)
        block_sin = lax.dynamic_slice_in_dim(full_sin, offset, line_count, 1)
        return (carried + predict(block_lines, block_cos, block_sin, own_cos, own_sin), None)

    summed, _ = lax.scan(one_block, zero_rows, (blocks, offsets))
    predicted = summed * (1.0 / math.sqrt(L * M))
    return weight.astype(jnp.float32)[:, None, :] * (visibility.astype(jnp.float32) - predicted)


def solution(mesh):
    return jax.shard_map(
        local,
        mesh=mesh,
        in_specs=(P("tile", None, "chan"), P("tile", "chan"), P(), P(), P()),
        out_specs=P("tile", None, "chan"),
        check_vma=False,
    )
```

profile of v0, /device:TPU:0, one launch (start us, length us, event | category | flops | bytes accessed | tf_op | source)
XLA Modules:
  0.0 1037.5 jit_solution(1772755833792879278)
XLA Ops:
  6.5 1.7 fusion.71
  8.3 1.6 copy_multiply_fusion
  10.0 0.8 broadcast_multiply_fusion
  10.7 8.2 fusion.57
  18.9 34.4 %fusion.32 = (f32[1024,64,32]{0,2,1:T(8,128)}, f32[1024,64,32]{0,2,1:T(8,128)}) fusion(s32[32]{0:T(128)S(1)} %multiply_add_fusion, s32[1024,64]{0,1:T(8,128)S(1)} %broadcast_multiply_fusion), kind=kLoop, calls=%fused_computation.55 | loop fusion | flops 29360128 | bytes 17039488 | tf_op jit(solution)/shard_map/cos | solution.py:31
  53.4 27.3 %add_convert_fusion.1 = (bf16[1024,64,32,8]{0,3,2,1:T(8,128)(2,1)}, bf16[1024,64,32,8]{0,3,2,1:T(8,128)(2,1)}) fusion(f32[1024,64,8]{0,2,1:T(8,128)S(1)} %get-tuple-element.152, f32[1024,64,32]{0,2,1:T(8,128)} %get-tuple-element.148, f32[1024,64,8]{0,2,1:T(8,128)S(1)} %get-tuple-element.151, f32[1024,64,32]{0,2,1:T(8,128)} %get-tuple-element.147), kind=kLoop, calls=%fused_computation.30 | loop fusion | flops 134217728 | bytes 88080384 | tf_op jit(solution)/shard_map/convert_element_type | solution.py:40
  80.7 5.0 cosine_convert_fusion
  85.6 5.5 fusion.61
  91.2 2.7 fusion.63
  93.8 1.6 copy.23
  95.4 2.5 copy.24
  97.9 46.6 %fusion.10 = (bf16[1024,16384]{0,1:T(8,128)(2,1)}, bf16[1024,16384]{0,1:T(8,128)(2,1)}) fusion(bf16[1024,64,32,8]{0,3,2,1:T(8,128)(2,1)} %get-tuple-element.144, bf16[1024,64,32,8]{0,3,2,1:T(8,128)(2,1)} %get-tuple-element.143, f32[1024,256]{0,1:T(8,128)} %copy.24, f32[1024,256]{0,1:T(8,128)S(1)} %copy.23), kind=kLoop, calls=%fused_computation.22 | loop fusion | flops 167772160 | bytes 136314880 | tf_op jit(solution)/shard_map/convert_element_type | solution.py:81
  144.5 28.8 %fusion.22 = bf16[16384,256]{1,0:T(8,128)(2,1)} fusion(bf16[1024,16384]{0,1:T(8,128)(2,1)} %get-tuple-element.140, bf16[1024,16384]{0,1:T(8,128)(2,1)} %get-tuple-element.139, bf16[1024,256]{1,0:T(8,128)(2,1)} %fusion.61, bf16[1024,256]{1,0:T(8,128)(2,1)} %cosine_convert_fusion), kind=kOutput, calls=%fused_computation.36 | convolution fusion | flops 17324572672 | bytes 76546048 | tf_op jit(solution)/shard_map/dot_general | solution.py:85
  173.3 192.2 %all_to_all.36 = bf16[64,256,256]{2,1,0:T(8,128)(2,1)} all-to-all(bf16[64,256,256]{2,1,0:T(8,128)(2,1)} %bitcast.133), channel_id=1, replica_groups=mesh['chan'=4,'tile'=8] {'chan'}, dimensions={0} | all-to-all | bytes 16777216 | tf_op jit(solution)/shard_map/all_to_all | solution.py:96
  365.5 13.7 %copy.25 = bf16[4,16,256,256]{2,0,3,1:T(4,128)(2,1)} copy(bf16[4,16,256,256]{3,2,1,0:T(8,128)(2,1)} %bitcast.129) | data formatting | bytes 16777216 | tf_op jit(solution)/shard_map/all_to_all | solution.py:96
  379.1 14.3 %all_to_all.29 = bf16[16,1024,256]{1,2,0:T(8,128)(2,1)} reshape(bf16[16,4,256,256]{2,1,3,0:T(4,128)(2,1)} %bitcast.130) | data formatting | bytes 16777216 | tf_op jit(solution)/shard_map/all_to_all | solution.py:96
  393.5 14.6 %convert_bitcast_fusion = bf16[16,1024,256]{1,2,0:T(8,128)(2,1)} fusion(bf16[16,1024,256]{1,2,0:T(8,128)(2,1)} %all_to_all.29, bf16[1024,1024]{1,0:T(8,128)(2,1)S(1)} %copy-done), kind=kOutput, calls=%fused_computation.53 | convolution fusion | flops 8594128896 | bytes 18874368 | tf_op jit(solution)/shard_map/fg,qgm->qfm/dot_general | solution.py:93
  408.1 12.6 %copy.26 = bf16[16,1024,256]{2,0,1:T(8,128)(2,1)} copy(bf16[16,1024,256]{1,2,0:T(8,128)(2,1)} %convert_bitcast_fusion) | data formatting | bytes 16777216 | tf_op jit(solution)/shard_map/convert_element_type | solution.py:98
  420.7 190.4 %all_to_all.37 = bf16[16,1024,256]{2,0,1:T(8,128)(2,1)} all-to-all(bf16[16,1024,256]{2,0,1:T(8,128)(2,1)} %copy.26), channel_id=1, replica_groups=mesh['chan'=4,'tile'=8] {'chan'}, dimensions={1} | all-to-all | bytes 16777216 | tf_op jit(solution)/shard_map/all_to_all | solution.py:99
  611.1 9.9 copy.28
  621.1 0.8 dynamic_slice.28
  622.6 8.2 fusion.59
  630.8 34.7 %fusion.34 = (f32[128,512,32]{0,2,1:T(8,128)}, f32[128,512,32]{0,2,1:T(8,128)}) fusion(s32[32]{0:T(128)S(1)} %copy-done.6, s32[128,512]{0,1:T(8,128)S(1)} %iota_multiply_fusion), kind=kLoop, calls=%fused_computation.57 | loop fusion | flops 29360128 | bytes 17039488 | tf_op jit(solution)/shard_map/cos | solution.py:31
  665.5 27.5 %fusion.18 = (bf16[128,512,256]{0,2,1:T(8,128)(2,1)}, bf16[128,512,256]{0,2,1:T(8,128)(2,1)}) fusion(f32[128,512,8]{0,2,1:T(8,128)S(1)} %get-tuple-element.154, f32[128,512,32]{0,2,1:T(8,128)} %get-tuple-element.150, f32[128,512,8]{0,2,1:T(8,128)S(1)} %get-tuple-element.153, f32[128,512,32]{0,2,1:T(8,128)} %get-tuple-element.149), kind=kLoop, calls=%fused_computation.34 | loop fusion | flops 134217728 | bytes 88080384 | tf_op jit(solution)/shard_map/convert_element_type | solution.py:40
  693.0 229.7 %all-gather.5.cloned.1.call-done = bf16[512,256,256]{2,1,0:T(8,128)(2,1)} async-done(((bf16[64,256,256]{2,1,0:T(8,128)(2,1)}), bf16[512,256,256]{2,1,0:T(8,128)(2,1)}) %all-gather.5.cloned.1.call-update) | async-done | bytes 67108880 | tf_op jit(solution)/shard_map/all_gather | solution.py:108
  922.7 106.0 %while.13 = (s32[]{:T(128)}, f32[128,2,256]{0,2,1:T(8,128)S(1)}, s32[8]{0:T(128)S(1)}, bf16[128,512,256]{0,2,1:T(8,128)(2,1)}, bf16[8,64,256,256]{3,2,1,0:T(8,12...) while((s32[]{:T(128)}, f32[128,2,256]{0,2,1:T(8,128)S(1)}, ...), condition=%wide.region_3.4_spmd.clone, body=%wide.region_0.3_spmd.clone.sunk | while | flops 2168619008 | bytes 51774108 | solution.py:120
  925.4 4.8 fusion.84
  930.2 5.6 fusion.85
  935.9 0.7 dynamic_slice.49
  938.6 4.8 fusion.84
  943.4 5.6 fusion.85
  949.2 0.7 dynamic_slice.49
  951.9 4.8 fusion.84
  956.7 5.6 fusion.85
  962.5 0.7 dynamic_slice.49
  965.1 4.8 fusion.84
  970.0 5.6 fusion.85
  975.7 0.7 dynamic_slice.49
  978.4 4.8 fusion.84
  983.2 5.6 fusion.85
  989.0 0.7 dynamic_slice.49
  991.7 4.8 fusion.84
  996.5 5.6 fusion.85
  1004.9 4.8 fusion.84
  1009.7 5.6 fusion.85
  1018.2 4.8 fusion.84
  1023.0 5.6 fusion.85
  1028.9 0.9 subtract_multiply_fusion
  (47 shorter events, 4.2 us)
Async XLA Ops:
  6.5 387.0 %copy-start = (bf16[1024,1024]{1,0:T(8,128)(2,1)S(1)}, bf16[1024,1024]{1,0:T(8,128)(2,1)}, u32[]{:S(2)}) copy-start(bf16[1024,1024]{1,0:T(8,128)(2,1)} %param.11) | copy-start | bytes 6291460
  6.5 84.6 %all-gather.3.cloned.1.call-start = ((), (), s32[]{:S(2)}) async-start(), calls=%async_computation.2 | async-start | bytes 1179648 | tf_op jit(solution)/shard_map/all_gather | solution.py:75
  9.9 912.8 %all-gather.5.cloned.1.call-start = ((), (), s32[]{:S(2)}) async-start(), calls=%async_computation.3 | async-start | bytes 75497472 | tf_op jit(solution)/shard_map/all_gather | solution.py:108
  9.9 43.4 %copy-start.5 = (s32[32]{0:T(128)}, s32[32]{0:T(128)S(1)}, u32[]{:S(2)}) copy-start(s32[32]{0:T(128)S(1)} %multiply_add_fusion) | copy-start | bytes 388
  53.4 27.3 %copy-start.4 = (s32[1024]{0:T(1024)S(1)}, s32[1024]{0:T(1024)}, u32[]{:S(2)}) copy-start(s32[1024]{0:T(1024)} %param.10) | copy-start | bytes 12292
  621.0 9.7 copy-start.6
  922.7 106.2 %copy-start.2 = (bf16[128,2,256]{2,1,0:T(2,128)(2,1)S(1)}, bf16[128,2,256]{2,1,0:T(2,128)(2,1)}, u32[]{:S(2)}) copy-start(bf16[128,2,256]{2,1,0:T(2,128)(2,1)} %param.7) | copy-start | bytes 393220
  922.7 106.2 %copy-start.3 = (f32[128,256]{1,0:T(8,128)S(1)}, f32[128,256]{1,0:T(8,128)}, u32[]{:S(2)}) copy-start(f32[128,256]{1,0:T(8,128)} %get-tuple-element.137) | copy-start | bytes 393220
  1028.7 1.7 copy-start.1
Sparse Core Ops, SparseCore 0:
  10.0 26.2 all-gather.2
  621.2 301.4 all-gather.4
where the time goes:
time: 1050 us; the launch traced here: 1040 us
  blocking collectives  383 us (36%)
  other arithmetic  251 us (24%)
  waiting for transfers between devices  230 us (22%)
  matrix products  81.8 us (8%)
  local copies, waits for them, and re-layouts  61.4 us (6%)
  loops' own time  16.6 us (2%)
  between operations  13.8 us (1%)
    all_gather x1, waiting for transfers between devices, local(): shard_piece = lax.all_gather(foreground, 'tile', axis=0, tiled=True)  230 us
    all_to_all x1, blocking collectives, local(): lax.all_to_all(dirty_image, 'chan', split_axis=0, concat_axis=1, tiled=True)  192 us
    all_to_all x1, blocking collectives, local(): lax.all_to_all(filtered, 'chan', split_axis=1, concat_axis=0, tiled=True)  190 us
    cos x2, other arithmetic, line_tables(): coarse_cos = jnp.cos(coarse_angle)[:, :, :, None]  69.1 us
    convert_element_type x2, other arithmetic, line_tables(): whole_sin.reshape(shape).astype(jnp.bfloat16)  54.8 us
    convert_element_type x1, other arithmetic, local(): x_real = (real_part * line_cos - imag_part * line_sin).astype(jnp.bfloat16)  46.6 us
    reduce_sum x8, other arithmetic, predict(): real_pred = jnp.sum(row_cos * half_cos - row_sin * half_sin, axis=0)  45 us
    dot_general x8, matrix products, predict(): lax.dot_general(image_lines.reshape(line_count * chan_count, pixel_cols),...  38.5 us
  transfers between devices with their start and end apart: 2, of which 1 were waited for; matrix products, arithmetic and copies ran while one was open for 15% of the time, Pallas kernels for 0%

commit v1 on v0

--- a/solution.py
+++ b/solution.py
@@ -9,6 +9,16 @@
 M = 256
 TWO_PI = 2.0 * math.pi
 FINE_STEP = 8
+
+
+def collect(x, axis, dim):
+    ways, here, step = (lax.axis_size(axis), lax.axis_index(axis), x.shape[dim])
+    shape = [n * ways if d == dim else n for d, n in enumerate(x.shape)]
+    full = lax.dynamic_update_slice_in_dim(jnp.zeros(shape, x.dtype), x, here * step, axis=dim)
+    for far in range(1, ways):
+        x = lax.ppermute(x, axis, [(d, (d + 1) % ways) for d in range(ways)])
+        full = lax.dynamic_update_slice_in_dim(full, x, (here - far) % ways * step, axis=dim)
+    return full
 
 
 def tables(grid_index, positions, period):
@@ -105,7 +115,7 @@
     )
     own_cos, own_sin = tables(v_owned, jnp.arange(M, dtype=jnp.int32), 2 * M)
     zero_rows = jnp.zeros((row_count, 2, chan_count), jnp.float32)
-    shard_piece = lax.all_gather(foreground, "tile", axis=0, tiled=True)
+    shard_piece = collect(foreground, "tile", 0)
     piece_lines = shard_piece.shape[0]
     block_count = piece_lines // line_count
     blocks = shard_piece.reshape(block_count, line_count, chan_count, M)

time: 1050 us -> 1440 us (1.37)
  waiting for transfers between devices: 230 us -> 527 us
  local copies, waits for them, and re-layouts: 61.4 us -> 156 us
    ppermute x0 -> x7, waiting for transfers between devices: none -> 527 us  [collect(): x = lax.ppermute(x, axis, [(d, (d + 1) % ways) for d in range(ways)])]
    all_gather x1 -> x0, waiting for transfers between devices: 230 us -> none  [local(): shard_piece = lax.all_gather(foreground, 'tile', axis=0, tiled=True)]
    dynamic_update_slice x0 -> x8, local copies, waits for them, and re-layouts: none -> 60.9 us  [the longest x7 53.3 us: collect(): lax.dynamic_update_slice_in_dim(full, x, (here - far) % ways * step, axis...]
    broadcast_in_dim x0 -> x1, local copies, waits for them, and re-layouts: none -> 20.9 us  [collect(): jnp.zeros(shape, x.dtype)]
  transfers between devices with their start and end apart: 2 -> 8, of which waited for: 1 -> 6; matrix products, arithmetic and copies ran while one was open for 15% -> 16% of each run, Pallas kernels for 0% -> 0%
where the time goes in v1:
time: 1440 us; the launch traced here: 1430 us
  waiting for transfers between devices  527 us (37%)
  blocking collectives  383 us (27%)
  other arithmetic  251 us (17%)
  local copies, waits for them, and re-layouts  156 us (11%)
  matrix products  81.9 us (6%)
    ppermute x7, waiting for transfers between devices, collect(): x = lax.ppermute(x, axis, [(d, (d + 1) % ways) for d in range(ways)])  527 us
    all_to_all x1, blocking collectives, local(): lax.all_to_all(dirty_image, 'chan', split_axis=0, concat_axis=1, tiled=True)  192 us
    all_to_all x1, blocking collectives, local(): lax.all_to_all(filtered, 'chan', split_axis=1, concat_axis=0, tiled=True)  190 us
    cos x2, other arithmetic, line_tables(): coarse_cos = jnp.cos(coarse_angle)[:, :, :, None]  69.1 us
    convert_element_type x2, other arithmetic, line_tables(): whole_sin.reshape(shape).astype(jnp.bfloat16)  54.8 us
    dynamic_update_slice x7, local copies, waits for them, and re-layouts, collect(): lax.dynamic_update_slice_in_dim(full, x, (here - far) % ways * step, axis...  53.3 us
    convert_element_type x1, other arithmetic, local(): x_real = (real_part * line_cos - imag_part * line_sin).astype(jnp.bfloat16)  46.6 us
    reduce_sum x8, other arithmetic, predict(): real_pred = jnp.sum(row_cos * half_cos - row_sin * half_sin, axis=0)  45 us
  transfers between devices with their start and end apart: 8, of which 6 were waited for; matrix products, arithmetic and copies ran while one was open for 16% of the time, Pallas kernels for 0%

profile of v1, /device:TPU:0, one launch (start us, length us, event | category | flops | bytes accessed | tf_op | source)
XLA Modules:
  0.0 1426.6 jit_solution(1274177761151785429)
XLA Ops:
  10.7 8.2 fusion.57
  18.9 34.4 %fusion.32 = (f32[1024,64,32]{0,2,1:T(8,128)}, f32[1024,64,32]{0,2,1:T(8,128)}) fusion(s32[32]{0:T(128)S(1)} %multiply_add_fusion, s32[1024,64]{0,1:T(8,128)S(1)} %broadcast_multiply_fusion), kind=kLoop, calls=%fused_computation.55 | loop fusion | flops 29360128 | bytes 17039488 | tf_op jit(solution)/shard_map/cos | solution.py:41
  53.3 27.3 %add_convert_fusion.1 = (bf16[1024,64,32,8]{0,3,2,1:T(8,128)(2,1)}, bf16[1024,64,32,8]{0,3,2,1:T(8,128)(2,1)}) fusion(f32[1024,64,8]{0,2,1:T(8,128)S(1)} %get-tuple-element.152, f32[1024,64,32]{0,2,1:T(8,128)} %get-tuple-element.148, f32[1024,64,8]{0,2,1:T(8,128)S(1)} %get-tuple-element.151, f32[1024,64,32]{0,2,1:T(8,128)} %get-tuple-element.147), kind=kLoop, calls=%fused_computation.30 | loop fusion | flops 134217728 | bytes 88080384 | tf_op jit(solution)/shard_map/convert_element_type | solution.py:50
  80.6 5.0 cosine_convert_fusion
  85.6 5.2 fusion.61
  97.6 46.6 %fusion.10 = (bf16[1024,16384]{0,1:T(8,128)(2,1)}, bf16[1024,16384]{0,1:T(8,128)(2,1)}) fusion(bf16[1024,64,32,8]{0,3,2,1:T(8,128)(2,1)} %get-tuple-element.144, bf16[1024,64,32,8]{0,3,2,1:T(8,128)(2,1)} %get-tuple-element.143, f32[1024,256]{0,1:T(8,128)} %copy.24, f32[1024,256]{0,1:T(8,128)S(1)} %copy.23), kind=kLoop, calls=%fused_computation.22 | loop fusion | flops 167772160 | bytes 136314880 | tf_op jit(solution)/shard_map/convert_element_type | solution.py:91
  144.2 28.8 %fusion.22 = bf16[16384,256]{1,0:T(8,128)(2,1)} fusion(bf16[1024,16384]{0,1:T(8,128)(2,1)} %get-tuple-element.140, bf16[1024,16384]{0,1:T(8,128)(2,1)} %get-tuple-element.139, bf16[1024,256]{1,0:T(8,128)(2,1)} %fusion.61, bf16[1024,256]{1,0:T(8,128)(2,1)} %cosine_convert_fusion), kind=kOutput, calls=%fused_computation.36 | convolution fusion | flops 17324572672 | bytes 76546048 | tf_op jit(solution)/shard_map/dot_general | solution.py:95
  173.0 192.4 %all_to_all.36 = bf16[64,256,256]{2,1,0:T(8,128)(2,1)} all-to-all(bf16[64,256,256]{2,1,0:T(8,128)(2,1)} %bitcast.134), channel_id=1, replica_groups=mesh['chan'=4,'tile'=8] {'chan'}, dimensions={0} | all-to-all | bytes 16777216 | tf_op jit(solution)/shard_map/all_to_all | solution.py:106
  365.4 13.7 copy.25
  379.1 14.4 %all_to_all.29 = bf16[16,1024,256]{1,2,0:T(8,128)(2,1)} reshape(bf16[16,4,256,256]{2,1,3,0:T(4,128)(2,1)} %bitcast.131) | data formatting | bytes 16777216 | tf_op jit(solution)/shard_map/all_to_all | solution.py:106
  393.4 14.7 %convert_bitcast_fusion = bf16[16,1024,256]{1,2,0:T(8,128)(2,1)} fusion(bf16[16,1024,256]{1,2,0:T(8,128)(2,1)} %all_to_all.29, bf16[1024,1024]{1,0:T(8,128)(2,1)S(1)} %copy-done), kind=kOutput, calls=%fused_computation.53 | convolution fusion | flops 8594128896 | bytes 18874368 | tf_op jit(solution)/shard_map/fg,qgm->qfm/dot_general | solution.py:103
  408.1 12.6 copy.26
  420.7 190.2 %all_to_all.37 = bf16[16,1024,256]{2,0,1:T(8,128)(2,1)} all-to-all(bf16[16,1024,256]{2,0,1:T(8,128)(2,1)} %copy.26), channel_id=1, replica_groups=mesh['chan'=4,'tile'=8] {'chan'}, dimensions={1} | all-to-all | bytes 16777216 | tf_op jit(solution)/shard_map/all_to_all | solution.py:109
  610.9 9.9 copy.28
  620.8 94.0 %collective-permute-done = bf16[64,256,256]{2,1,0:T(8,128)(2,1)S(1)} collective-permute-done((bf16[64,256,256]{2,1,0:T(8,128)(2,1)}, bf16[64,256,256]{2,1,0:T(8,128)(2,1)S(1)}, u32[]{:S(2)}, u32[]{:S(2)}) %collective-permute-start) | collective-permute-done | bytes 8388640 | tf_op jit(solution)/shard_map/ppermute | solution.py:19
  718.0 93.8 %collective-permute-done.1 = bf16[64,256,256]{2,1,0:T(8,128)(2,1)S(1)} collective-permute-done((bf16[64,256,256]{2,1,0:T(8,128)(2,1)S(1)}, bf16[64,256,256]{2,1,0:T(8,128)(2,1)S(1)}, u32[]{:S(2)}, u32[]{:S(2)}) %collective-permute-start.1) | collective-permute-done | bytes 8388640 | tf_op jit(solution)/shard_map/ppermute | solution.py:19
  815.0 93.8 %collective-permute-done.2 = bf16[64,256,256]{2,1,0:T(8,128)(2,1)S(1)} collective-permute-done((bf16[64,256,256]{2,1,0:T(8,128)(2,1)S(1)}, bf16[64,256,256]{2,1,0:T(8,128)(2,1)S(1)}, u32[]{:S(2)}, u32[]{:S(2)}) %collective-permute-start.2) | collective-permute-done | bytes 8388640 | tf_op jit(solution)/shard_map/ppermute | solution.py:19
  912.0 93.8 %collective-permute-done.3 = bf16[64,256,256]{2,1,0:T(8,128)(2,1)S(1)} collective-permute-done((bf16[64,256,256]{2,1,0:T(8,128)(2,1)S(1)}, bf16[64,256,256]{2,1,0:T(8,128)(2,1)S(1)}, u32[]{:S(2)}, u32[]{:S(2)}) %collective-permute-start.3) | collective-permute-done | bytes 8388640 | tf_op jit(solution)/shard_map/ppermute | solution.py:19
  1009.0 93.9 %collective-permute-done.4 = bf16[64,256,256]{2,1,0:T(8,128)(2,1)} collective-permute-done((bf16[64,256,256]{2,1,0:T(8,128)(2,1)S(1)}, bf16[64,256,256]{2,1,0:T(8,128)(2,1)}, u32[]{:S(2)}, u32[]{:S(2)}) %collective-permute-start.4) | collective-permute-done | bytes 8388640 | tf_op jit(solution)/shard_map/ppermute | solution.py:19
  1104.4 34.7 %fusion.34 = (f32[128,512,32]{0,2,1:T(8,128)}, f32[128,512,32]{0,2,1:T(8,128)}) fusion(s32[32]{0:T(128)S(1)} %copy-done.10, s32[128,512]{0,1:T(8,128)S(1)} %iota_multiply_fusion), kind=kLoop, calls=%fused_computation.57 | loop fusion | flops 29360128 | bytes 17039488 | tf_op jit(solution)/shard_map/cos | solution.py:41
  1139.1 57.9 %collective-permute-done.5 = bf16[64,256,256]{2,1,0:T(8,128)(2,1)} collective-permute-done((bf16[64,256,256]{2,1,0:T(8,128)(2,1)}, bf16[64,256,256]{2,1,0:T(8,128)(2,1)}, u32[]{:S(2)}, u32[]{:S(2)}) %collective-permute-start.5) | collective-permute-done | bytes 8388640 | tf_op jit(solution)/shard_map/ppermute | solution.py:19
  1197.0 8.2 fusion.59
  1205.2 27.5 %fusion.18 = (bf16[128,512,256]{0,2,1:T(8,128)(2,1)}, bf16[128,512,256]{0,2,1:T(8,128)(2,1)}) fusion(f32[128,512,8]{0,2,1:T(8,128)S(1)} %get-tuple-element.154, f32[128,512,32]{0,2,1:T(8,128)} %get-tuple-element.150, f32[128,512,8]{0,2,1:T(8,128)S(1)} %get-tuple-element.153, f32[128,512,32]{0,2,1:T(8,128)} %get-tuple-element.149), kind=kLoop, calls=%fused_computation.34 | loop fusion | flops 134217728 | bytes 88080384 | tf_op jit(solution)/shard_map/convert_element_type | solution.py:50
  1232.7 20.9 %broadcast_in_dim.5 = bf16[512,256,256]{2,1,0:T(8,128)(2,1)} broadcast(bf16[]{:T(256)} %constant.152.clone.1), dimensions={} | broadcast | bytes 67108864 | tf_op jit(solution)/shard_map/broadcast_in_dim | solution.py:17
  1253.6 7.6 constant_dynamic-update-slice_fusion.7
  1261.3 7.6 constant_dynamic-update-slice_fusion.6
  1268.8 7.6 constant_dynamic-update-slice_fusion.5
  1276.5 7.6 constant_dynamic-update-slice_fusion.4
  1284.1 7.6 constant_dynamic-update-slice_fusion.3
  1291.7 7.6 constant_dynamic-update-slice_fusion.2
  1299.3 7.6 constant_dynamic-update-slice_fusion.1
  1306.9 7.6 constant_dynamic-update-slice_fusion
  1314.5 103.0 %while.13 = (s32[]{:T(128)}, f32[128,2,256]{0,2,1:T(8,128)S(1)}, s32[8]{0:T(128)S(1)}, bf16[128,512,256]{0,2,1:T(8,128)(2,1)}, bf16[8,64,256,256]{3,2,1,0:T(8,12...) while((s32[]{:T(128)}, f32[128,2,256]{0,2,1:T(8,128)S(1)}, ...), condition=%wide.region_3.4_spmd.clone, body=%wide.region_0.3_spmd.clone.sunk | while | flops 2168619008 | bytes 51774108 | solution.py:130
  1317.1 4.8 fusion.84
  1321.9 5.6 fusion.85
  1329.9 4.8 fusion.84
  1334.7 5.6 fusion.85
  1342.8 4.8 fusion.84
  1347.6 5.6 fusion.85
  1355.6 4.8 fusion.84
  1360.4 5.6 fusion.85
  1368.5 4.8 fusion.84
  1373.3 5.6 fusion.85
  1381.3 4.8 fusion.84
  1386.1 5.6 fusion.85
  1394.2 4.8 fusion.84
  1399.0 5.6 fusion.85
  1411.8 5.6 fusion.85
  (75 shorter events, 37.2 us)
Async XLA Ops:
  6.5 386.9 %copy-start = (bf16[1024,1024]{1,0:T(8,128)(2,1)S(1)}, bf16[1024,1024]{1,0:T(8,128)(2,1)}, u32[]{:S(2)}) copy-start(bf16[1024,1024]{1,0:T(8,128)(2,1)} %param.11) | copy-start | bytes 6291460
  6.5 84.3 %all-gather.2.cloned.1.call-start = ((), (), s32[]{:S(2)}) async-start(), calls=%async_computation.2 | async-start | bytes 1179648 | tf_op jit(solution)/shard_map/all_gather | solution.py:85
  9.9 43.4 %copy-start.9 = (s32[32]{0:T(128)}, s32[32]{0:T(128)S(1)}, u32[]{:S(2)}) copy-start(s32[32]{0:T(128)S(1)} %multiply_add_fusion) | copy-start | bytes 388
  53.3 27.3 %copy-start.8 = (s32[1024]{0:T(1024)S(1)}, s32[1024]{0:T(1024)}, u32[]{:S(2)}) copy-start(s32[1024]{0:T(1024)} %param.10) | copy-start | bytes 12292
  610.8 493.5 %copy-start.10 = (s32[32]{0:T(128)S(1)}, s32[32]{0:T(128)}, u32[]{:S(2)}) copy-start(s32[32]{0:T(128)} %copy-done.9) | copy-start | bytes 388
  620.8 94.0 %collective-permute-start = (bf16[64,256,256]{2,1,0:T(8,128)(2,1)}, bf16[64,256,256]{2,1,0:T(8,128)(2,1)S(1)}, u32[]{:S(2)}, u32[]{:S(2)}) collective-permute-start(bf16[64,256,256]{2,1,0:T(8,128)(2,1)} %bitcast.128), channel_id=1, source_target_pairs={{0,1},{1,2},{2,3},{3,4},{4,5},{5,6},{6,7},{7,0},{8,9},{9,10},{10,1... | collective-permute-start | bytes 25165832 | tf_op jit(solution)/shard_map/ppermute | solution.py:19
  714.8 3.2 copy-start.2
  718.0 93.8 %collective-permute-start.1 = (bf16[64,256,256]{2,1,0:T(8,128)(2,1)S(1)}, bf16[64,256,256]{2,1,0:T(8,128)(2,1)S(1)}, u32[]{:S(2)}, u32[]{:S(2)}) collective-permute-start(bf16[64,256,256]{2,1,0:T(8,128)(2,1)S(1)} %collective-permute-done), channel_id=1, source_target_pairs={{0,1},{1,2},{2,3},{3,4},{4,5},{5,6},{6,7},{7,0},{8,9},{9,10},{10,1... | collective-permute-start | bytes 25165832 | tf_op jit(solution)/shard_map/ppermute | solution.py:19
  811.8 3.2 copy-start.3
  815.0 93.8 %collective-permute-start.2 = (bf16[64,256,256]{2,1,0:T(8,128)(2,1)S(1)}, bf16[64,256,256]{2,1,0:T(8,128)(2,1)S(1)}, u32[]{:S(2)}, u32[]{:S(2)}) collective-permute-start(bf16[64,256,256]{2,1,0:T(8,128)(2,1)S(1)} %collective-permute-done.1), channel_id=1, source_target_pairs={{0,1},{1,2},{2,3},{3,4},{4,5},{5,6},{6,7},{7,0},{8,9},{9,10},{10,1... | collective-permute-start | bytes 25165832 | tf_op jit(solution)/shard_map/ppermute | solution.py:19
  908.8 3.2 copy-start.4
  912.0 93.8 %collective-permute-start.3 = (bf16[64,256,256]{2,1,0:T(8,128)(2,1)S(1)}, bf16[64,256,256]{2,1,0:T(8,128)(2,1)S(1)}, u32[]{:S(2)}, u32[]{:S(2)}) collective-permute-start(bf16[64,256,256]{2,1,0:T(8,128)(2,1)S(1)} %collective-permute-done.2), channel_id=1, source_target_pairs={{0,1},{1,2},{2,3},{3,4},{4,5},{5,6},{6,7},{7,0},{8,9},{9,10},{10,1... | collective-permute-start | bytes 25165832 | tf_op jit(solution)/shard_map/ppermute | solution.py:19
  1005.8 3.2 copy-start.5
  1009.0 93.9 %collective-permute-start.4 = (bf16[64,256,256]{2,1,0:T(8,128)(2,1)S(1)}, bf16[64,256,256]{2,1,0:T(8,128)(2,1)}, u32[]{:S(2)}, u32[]{:S(2)}) collective-permute-start(bf16[64,256,256]{2,1,0:T(8,128)(2,1)S(1)} %collective-permute-done.3), channel_id=1, source_target_pairs={{0,1},{1,2},{2,3},{3,4},{4,5},{5,6},{6,7},{7,0},{8,9},{9,10},{10,1... | collective-permute-start | bytes 25165832 | tf_op jit(solution)/shard_map/ppermute | solution.py:19
  1102.9 94.1 %collective-permute-start.5 = (bf16[64,256,256]{2,1,0:T(8,128)(2,1)}, bf16[64,256,256]{2,1,0:T(8,128)(2,1)}, u32[]{:S(2)}, u32[]{:S(2)}) collective-permute-start(bf16[64,256,256]{2,1,0:T(8,128)(2,1)} %collective-permute-done.4), channel_id=1, source_target_pairs={{0,1},{1,2},{2,3},{3,4},{4,5},{5,6},{6,7},{7,0},{8,9},{9,10},{10,1... | collective-permute-start | bytes 25165832 | tf_op jit(solution)/shard_map/ppermute | solution.py:19
  1197.0 110.0 %collective-permute-start.6 = (bf16[64,256,256]{2,1,0:T(8,128)(2,1)}, bf16[64,256,256]{2,1,0:T(8,128)(2,1)}, u32[]{:S(2)}, u32[]{:S(2)}) collective-permute-start(bf16[64,256,256]{2,1,0:T(8,128)(2,1)} %collective-permute-done.5), channel_id=1, source_target_pairs={{0,1},{1,2},{2,3},{3,4},{4,5},{5,6},{6,7},{7,0},{8,9},{9,10},{10,1... | collective-permute-start | bytes 25165832 | tf_op jit(solution)/shard_map/ppermute | solution.py:19
  1314.5 103.2 %copy-start.6 = (bf16[128,2,256]{2,1,0:T(2,128)(2,1)S(1)}, bf16[128,2,256]{2,1,0:T(2,128)(2,1)}, u32[]{:S(2)}) copy-start(bf16[128,2,256]{2,1,0:T(2,128)(2,1)} %param.7) | copy-start | bytes 393220
  1314.5 103.2 %copy-start.7 = (f32[128,256]{1,0:T(8,128)S(1)}, f32[128,256]{1,0:T(8,128)}, u32[]{:S(2)}) copy-start(f32[128,256]{1,0:T(8,128)} %get-tuple-element.137) | copy-start | bytes 393220
  1417.6 1.7 copy-start.1
Sparse Core Ops, SparseCore 0:
  10.0 26.2 all-gather.1
